TPU v7x, 32 devices: a whole 2x2x4 slice. The times are simulated.
32 devices in a mesh: groups: 2 (over y), dp: 4 (over x, core), member: 4 (over z).
Axes of the slice: x: 2, y: 2, z: 4, core: 2. Of those that a mesh axis runs over, the one named last changes fastest.
Arguments:
- context: bfloat16 [4096, 1024], P(('groups', 'dp', 'member')), parts along dimension 0, may hold values from -6 to 6
- residual: bfloat16 [4096, 1024], P(('groups', 'dp', 'member')), parts along dimension 0, may hold values from -6 to 6
- proj_weight: bfloat16 [1024, 1024], P('member'), may hold values from -0.1875 to 0.1875
- head_weights: bfloat16 [4, 1024, 1024], P('member'), may hold values from -0.1875 to 0.1875
- boot: int32 [128, 4], P(('groups', 'dp', 'member')), parts along dimension 0, may hold values from 0 to 4, as said below
Outputs:
- grad_context: bfloat16 [4096, 1024], P(('groups', 'dp', 'member')), parts along dimension 0
- grad_residual: bfloat16 [4096, 1024], P(('groups', 'dp', 'member')), parts along dimension 0
- grad_proj: float32 [2048, 1024], P(('groups', 'member')), parts along dimension 0
- grad_heads: float32 [8, 1024, 1024], P(('groups', 'member'), 'dp'), parts along dimension 0
There are 2 independent parts, one for each index of `groups`. A program takes and returns all parts, laid end to end along the dimension named above; an argument that names none is the same for every part. Nothing has to cross between parts.
Inputs may be any that keep to these rules, and one draw needn't show every extreme that they name: `boot`: among the 4 blocks of one device at most 2 have a nonzero weight for any one head. Every device has exactly 2 such blocks for some head, and in every draw some head gets exactly 2 from every device of one index of dp. Weights follow a Poisson law of mean one, cut at 4.
All inputs are finite; a program needn't handle non-finite values.
Results may differ from a plain program's by a relative error of at most 0.013.
Values may be sent and summed in bfloat16 or wider, within the bound.
A program may use at most 64 MiB of HBM per device.

v0:
```python
import jax
import jax.numpy as jnp
from jax import lax
from jax.sharding import PartitionSpec as P

POOL = 2
BLOCK = 16
BLK_DEV = 4
CAP = 2


EPS = 1e-06


def gelu_tanh(pre_value):
    return jax.nn.gelu(pre_value, approximate=True)


def slot_table(weights):
    live_mask = (weights > 0).astype(jnp.int32)
    live_rank = jnp.cumsum(live_mask, axis=-1) - 1
    slot_ids = jnp.arange(CAP, dtype=jnp.int32)
    picked = live_mask[..., None, :] * (live_rank[..., None, :] == slot_ids[:, None]).astype(
        jnp.int32
    )
    slot_weight = jnp.sum(picked * weights[..., None, :], axis=-1)
    return (picked, slot_weight)


def head_pass(block_rows, slot_weight, weight, head_count):
    block_rows = block_rows.astype(jnp.float32)
    model_width = block_rows.shape[-1]
    flat_rows = block_rows.reshape(-1, model_width)
    inverse = lax.rsqrt(jnp.mean(flat_rows * flat_rows, axis=-1, keepdims=True) + EPS)
    normed = flat_rows * inverse
    normed_low = normed.astype(jnp.bfloat16)
    pre_act = jnp.dot(normed_low, weight, preferred_element_type=jnp.float32)
    activated, back_act = jax.vjp(gelu_tanh, pre_act)
    pred = (flat_rows + activated).reshape(block_rows.shape)
    error_rows = pred[:, :, :-1] - block_rows[:, :, 1:]
    error_rows = jnp.concatenate([error_rows, jnp.zeros_like(error_rows[:, :, :1])], axis=2)
    row_scale = slot_weight.astype(jnp.float32) / head_count
    d_pred = (error_rows * row_scale[:, :, None, None]).reshape(flat_rows.shape)
    d_pre_low = back_act(d_pred)[0].astype(jnp.bfloat16)
    d_normed = lax.dot_general(
        d_pre_low, weight, (((1,), (1,)), ((), ())), preferred_element_type=jnp.float32
    )
    d_rows = d_pred + inverse * (
        d_normed - normed * jnp.mean(d_normed * normed, axis=-1, keepdims=True)
    )
    return (normed_low, d_pre_low, d_rows.astype(jnp.bfloat16).reshape(block_rows.shape))


def local(context, residual, proj_weight, head_weights, boot):
    members = lax.axis_size("member")
    head_count = boot.shape[1]
    model_width = context.shape[1]
    own_index = lax.axis_index("member")
    whole_proj = lax.all_gather(proj_weight, "member", axis=0, tiled=True)
    hidden = residual.astype(jnp.float32) + jnp.dot(
        context, whole_proj, preferred_element_type=jnp.float32
    )
    latent = jnp.mean(hidden.reshape(BLK_DEV * BLOCK, POOL, model_width), axis=1).astype(
        jnp.bfloat16
    )
    latent = latent.reshape(BLK_DEV, BLOCK, model_width)
    picked_out, weight_out = slot_table(boot.T)
    all_latent, all_boot = (
        lax.all_gather(latent, "member", axis=0, tiled=True),
        lax.all_gather(boot, "member", axis=0, tiled=True),
    )
    own_mask = (jnp.arange(head_count, dtype=jnp.int32) == own_index).astype(jnp.int32)
    column = jnp.sum(all_boot * own_mask[None, :], axis=1).reshape(members, BLK_DEV)
    picked_in, weight_in = slot_table(column)
    all_latent = all_latent.reshape(members, BLK_DEV, BLOCK, model_width)
    received = jnp.einsum(
        "jsk,jkrd->jsrd",
        picked_in.astype(jnp.bfloat16),
        all_latent,
        preferred_element_type=jnp.float32,
    ).astype(jnp.bfloat16)
    weight = head_weights[0]
    normed_low, d_pre_low, d_rows = head_pass(received, weight_in, weight, head_count)
    columns = normed_low
    grad_head = lax.psum_scatter(
        lax.dot_general(
            columns, d_pre_low, (((0,), (0,)), ((), ())), preferred_element_type=jnp.float32
        ).astype(jnp.bfloat16),
        "dp",
        scatter_dimension=0,
        tiled=True,
    ).astype(jnp.float32)
    returned = lax.all_to_all(d_rows, "member", split_axis=0, concat_axis=0, tiled=True)
    grad_latent = jnp.einsum(
        "hsk,hsrd->krd",
        picked_out.astype(jnp.bfloat16),
        returned,
        preferred_element_type=jnp.float32,
    )
    grad_tokens = jnp.broadcast_to(
        grad_latent.reshape(BLK_DEV * BLOCK, 1, model_width) / POOL,
        (BLK_DEV * BLOCK, POOL, model_width),
    )
    grad_low = grad_tokens.reshape(-1, model_width).astype(jnp.bfloat16)
    grad_context = lax.dot_general(
        grad_low, whole_proj, (((1,), (1,)), ((), ())), preferred_element_type=jnp.float32
    )
    columns = context
    grad_proj = lax.psum_scatter(
        lax.dot_general(
            columns, grad_low, (((0,), (0,)), ((), ())), preferred_element_type=jnp.float32
        ).astype(jnp.bfloat16),
        "member",
        scatter_dimension=0,
        tiled=True,
    ).astype(jnp.float32)
    grad_proj = lax.psum(grad_proj.astype(jnp.bfloat16), "dp").astype(jnp.float32)
    return (grad_context.astype(jnp.bfloat16), grad_low, grad_proj, grad_head[None])


def solution(mesh):
    in_specs = (
        P(("groups", "dp", "member"), None),
        P(("groups", "dp", "member"), None),
        P("member", None),
        P("member", None, None),
        P(("groups", "dp", "member"), None),
    )
    out_specs = (
        P(("groups", "dp", "member"), None),
        P(("groups", "dp", "member"), None),
        P(("groups", "member"), None),
        P(("groups", "member"), "dp", None),
    )
    return jax.shard_map(local, mesh=mesh, in_specs=in_specs, out_specs=out_specs, check_vma=False)
```

profile of v0, /device:TPU:1, one launch (start us, length us, event | category | flops | bytes accessed | tf_op | source)
XLA Modules:
  0.0 213.8 jit_solution(9833878894406099748)
XLA Ops:
  7.2 0.0 copy-start
  7.2 0.0 all-gather.3.cloned.1.call-start
  7.2 0.7 all-gather.3.cloned.1.call-update
  7.9 0.8 copy.59
  8.7 10.5 %all-gather = s32[4,4,4]{2,1,0:T(4,128)S(1)} all-gather(s32[1,4,4]{2,1,0:T(4,128)} %bitcast.80), channel_id=1, replica_groups=mesh['groups'=2,'dp'=4,'member'=4] {'member'}, dimensions={0}, use_global_device_ids=true | all-gather | bytes 320 | tf_op jit(solution)/shard_map/all_gather | solution.py:70
  19.2 0.1 copy.83
  19.3 0.1 multiply_reduce_fusion.2
  19.4 0.1 reshape.110
  19.5 0.1 copy.73
  19.6 0.1 copy.65
  19.6 0.2 reduce_window_sum.18
  19.8 0.1 copy.64
  20.0 0.1 copy.81
  20.1 0.1 copy.74
  20.2 37.0 %all-gather.3.cloned.1.call-done = bf16[1024,1024]{1,0:T(8,128)(2,1)} async-done(((bf16[256,1024]{1,0:T(8,128)(2,1)}), bf16[1024,1024]{1,0:T(8,128)(2,1)}) %all-gather.3.cloned.1.call-update) | async-done | bytes 2097168 | tf_op jit(solution)/shard_map/all_gather | solution.py:59
  57.1 2.1 convolution_add_fusion
  59.3 0.3 reshape.111
  59.6 0.6 reduce_sum.46
  60.2 12.5 %all_gather.11 = bf16[16,16,1024]{2,1,0:T(8,128)(2,1)S(1)} all-gather(bf16[4,16,1024]{2,1,0:T(8,128)(2,1)S(1)} %bitcast.76), channel_id=1, replica_groups=mesh['groups'=2,'dp'=4,'member'=4] {'member'}, dimensions={0}, use_global_device_ids=true | all-gather | bytes 655360 | tf_op jit(solution)/shard_map/all_gather | solution.py:69
  72.7 0.6 multiply_reduce_fusion.1
  73.4 0.2 copy.68
  73.5 0.1 copy.76
  73.6 0.2 multiply_convert_fusion
  73.9 0.1 rsqrt.13
  74.0 0.1 copy.71
  74.0 0.0 copy-done
  74.0 0.5 bitcast_add_fusion.1
  74.6 0.5 slice_subtract_fusion
  75.1 0.3 pad_multiply_fusion
  75.3 0.2 copy.75
  75.5 0.4 fusion.13
  75.9 0.9 multiply_reduce_fusion
  76.8 0.0 copy-start.2
  76.8 0.2 fusion.19
  77.0 1.0 copy.77
  78.0 3.4 %all-to-all-start = ((bf16[4,2,16,1024]{3,1,2,0:T(2,128)(2,1)}), bf16[4,2,16,1024]{3,1,2,0:T(2,128)(2,1)S(1)}, u32[]{:S(2)}, u32[]{:S(2)}) async-start(bf16[4,2,16,1024]{3,1,2,0:T(2,128)(2,1)} %copy.77), calls=%async_computation | async-start | bytes 524288 | tf_op jit(solution)/shard_map/all_to_all | solution.py:93
  81.4 0.0 reduce-scatter.3.cloned.1.call-start
  81.5 0.1 copy.61
  81.6 0.2 reduce_window_sum.17
  81.7 0.1 copy.60
  81.8 5.2 %all-to-all-done = bf16[4,2,16,1024]{3,1,2,0:T(2,128)(2,1)S(1)} async-done(((bf16[4,2,16,1024]{3,1,2,0:T(2,128)(2,1)}), bf16[4,2,16,1024]{3,1,2,0:T(2,128)(2,1)S(1)}, u32[]{:S(2)}, u32[]{:S(2)}) %all-to-all-start) | async-done | bytes 262176 | tf_op jit(solution)/shard_map/all_to_all | solution.py:93
  87.0 0.4 fusion.6
  87.5 0.1 broadcast_in_dim.7
  87.6 0.1 convert_element_type.115
  87.7 0.0 copy-done.2
  87.7 0.0 copy-start.1
  87.7 2.0 convert_bitcast_fusion
  89.8 0.0 reduce-scatter.3.cloned.1.call-update
  89.8 0.0 reduce-scatter.5.cloned.1.call-start
  89.8 2.1 convolution_convert_fusion
  91.9 0.0 reduce-scatter.5.cloned.1.call-update
  91.9 0.0 all-reduce.3.cloned.1.call-start
  92.0 0.0 copy-done.1
  92.0 3.1 %convolution_convert_fusion.1 = bf16[128,1024]{1,0:T(8,128)(2,1)} fusion(bf16[128,1024]{1,0:T(8,128)(2,1)S(1)} %convert_element_type.115, bf16[1024,1024]{1,0:T(8,128)(2,1)} %all-gather.3.cloned.1.call-done), kind=kOutput, calls=%fused_computation.7 | convolution fusion | flops 268566528 | bytes 2621440 | tf_op jit(solution)/shard_map/dot_general | solution.py:105
  95.1 42.2 %reduce-scatter.3.cloned.1.call-done = bf16[256,1024]{0,1:T(8,128)(2,1)} async-done(((bf16[1024,1024]{0,1:T(8,128)(2,1)}), bf16[256,1024]{0,1:T(8,128)(2,1)}) %reduce-scatter.3.cloned.1.call-update) | async-done | bytes 524304 | tf_op jit(solution)/shard_map/reduce_scatter | solution.py:109
  137.3 0.0 all-reduce.3.cloned.1.call-update
  137.3 33.1 %reduce-scatter.5.cloned.1.call-done = bf16[256,1024]{1,0:T(8,128)(2,1)} async-done(((bf16[1024,1024]{1,0:T(8,128)(2,1)}), bf16[256,1024]{1,0:T(8,128)(2,1)}) %reduce-scatter.5.cloned.1.call-update) | async-done | bytes 524304 | tf_op jit(solution)/shard_map/reduce_scatter | solution.py:85
  170.4 2.1 bitcast_convert_fusion
  172.6 32.5 %all-reduce.3.cloned.1.call-done = bf16[256,1024]{0,1:T(8,128)(2,1)} async-done(((bf16[256,1024]{0,1:T(8,128)(2,1)}), bf16[256,1024]{0,1:T(8,128)(2,1)}) %all-reduce.3.cloned.1.call-update) | async-done | bytes 524304 | tf_op jit(solution)/shard_map/psum | solution.py:117
  205.1 2.2 %copy.80 = f32[256,1024]{1,0:T(8,128)} copy(bf16[256,1024]{0,1:T(8,128)(2,1)} %all-reduce.3.cloned.1.call-done) | data formatting | bytes 1572864
  (11 shorter events, 0.1 us)
Async XLA Ops:
  7.2 66.9 %copy-start = (bf16[1,1024,1024]{2,1,0:T(8,128)(2,1)S(1)}, bf16[1,1024,1024]{2,1,0:T(8,128)(2,1)}, u32[]{:S(2)}) copy-start(bf16[1,1024,1024]{2,1,0:T(8,128)(2,1)} %param.8) | copy-start | bytes 6291460
  7.2 50.0 %all-gather.3.cloned.1.call-start = ((), (), s32[]{:S(2)}) async-start(), calls=%async_computation.3 | async-start | bytes 2621440 | tf_op jit(solution)/shard_map/all_gather | solution.py:59
  76.8 10.9 %copy-start.2 = (bf16[128,1024]{1,0:T(8,128)(2,1)S(1)}, bf16[128,1024]{1,0:T(8,128)(2,1)}, u32[]{:S(2)}) copy-start(bf16[128,1024]{1,0:T(8,128)(2,1)} %param.5) | copy-start | bytes 786436
  78.0 9.0 %all-to-all-start = ((bf16[4,2,16,1024]{3,1,2,0:T(2,128)(2,1)}), bf16[4,2,16,1024]{3,1,2,0:T(2,128)(2,1)S(1)}, u32[]{:S(2)}, u32[]{:S(2)}) async-start(bf16[4,2,16,1024]{3,1,2,0:T(2,128)(2,1)} %copy.77), calls=%async_computation | async-start | bytes 524288 | tf_op jit(solution)/shard_map/all_to_all | solution.py:93
  81.4 55.9 %reduce-scatter.3.cloned.1.call-start = ((), (), s32[]{:S(2)}) async-start(), calls=%async_computation.4 | async-start | bytes 2621440 | tf_op jit(solution)/shard_map/reduce_scatter | solution.py:109
  87.7 4.3 %copy-start.1 = (bf16[128,1024]{1,0:T(8,128)(2,1)}, bf16[128,1024]{1,0:T(8,128)(2,1)S(1)}, u32[]{:S(2)}) copy-start(bf16[128,1024]{1,0:T(8,128)(2,1)S(1)} %convert_element_type.115) | copy-start | bytes 786436
  89.8 80.6 %reduce-scatter.5.cloned.1.call-start = ((), (), s32[]{:S(2)}) async-start(), calls=%async_computation.6 | async-start | bytes 2621440 | tf_op jit(solution)/shard_map/reduce_scatter | solution.py:85
  91.9 113.1 %all-reduce.3.cloned.1.call-start = ((), (), s32[]{:S(2)}) async-start(), calls=%async_computation.5 | async-start | bytes 1048576 | tf_op jit(solution)/shard_map/psum | solution.py:117
Sparse Core Ops, SparseCore 0:
  9.6 47.5 all-gather.2
  89.9 47.3 reduce-scatter.2
  139.8 30.5 reduce-scatter.4
  172.6 32.4 all-reduce.2
where the time goes:
time: 216 us; the launch traced here: 214 us
  waiting for transfers between devices  151 us (70%)
  blocking collectives  23 us (11%)
  between operations  14 us (6%)
  matrix products  11.8 us (5%)
  local copies, waits for them, and re-layouts  5.98 us (3%)
  other arithmetic  4.83 us (2%)
  starting transfers between devices  3.57 us (2%)
    reduce_scatter x1, waiting for transfers between devices, local(): lax.psum_scatter(lax.dot_general(columns, grad_low, (((0,), (0,)), ((), (...  42.2 us
    all_gather x1, waiting for transfers between devices, local(): whole_proj = lax.all_gather(proj_weight, 'member', axis=0, tiled=True)  37 us
    reduce_scatter x1, waiting for transfers between devices, local(): lax.psum_scatter(lax.dot_general(columns, d_pre_low, (((0,), (0,)), ((),...  33.1 us
    psum x1, waiting for transfers between devices, local(): lax.psum(grad_proj.astype(jnp.bfloat16), 'dp').astype(jnp.float32)  32.5 us
    all_gather x1, blocking collectives, local(): lax.all_gather(latent, 'member', axis=0, tiled=True)  12.5 us
    all_gather x1, blocking collectives, local(): lax.all_gather(boot, 'member', axis=0, tiled=True)  10.5 us
    all_to_all x1, waiting for transfers between devices, local(): lax.all_to_all(d_rows, 'member', split_axis=0, concat_axis=0, tiled=True)  5.16 us
  transfers between devices with their start and end apart: 5, of which 5 were waited for; matrix products, arithmetic and copies ran while one was open for 4% of the time, Pallas kernels for 0%

commit v1 on v0

--- a/solution.py
+++ b/solution.py
@@ -1,6 +1,10 @@
+import functools
+
 import jax
 import jax.numpy as jnp
 from jax import lax
+from jax.experimental import pallas as pl
+from jax.experimental.pallas import tpu as pltpu
 from jax.sharding import PartitionSpec as P
 
 POOL = 2
@@ -53,6 +57,9 @@
 
 def local(context, residual, proj_weight, head_weights, boot):
     members = lax.axis_size("member")
+    fits = lax.axis_size("dp") == 4 and lax.axis_size("groups") == 2
+    if fits and boot.shape[1] == members and context.shape[1] % (256 * members) == 0:
+        return fused(context, residual, proj_weight, head_weights, boot)
     head_count = boot.shape[1]
     model_width = context.shape[1]
     own_index = lax.axis_index("member")
@@ -118,6 +125,292 @@
     return (grad_context.astype(jnp.bfloat16), grad_low, grad_proj, grad_head[None])
 
 
+MESH = pl.DeviceIdType.MESH
+F32 = jnp.float32
+BF16 = jnp.bfloat16
+LANES = 128
+ROW_DEV = BLK_DEV * BLOCK
+ROW_SLOT = CAP * BLOCK
+
+
+def picks(boot_ref, head):
+    weights = [boot_ref[k, head] for k in range(BLK_DEV)]
+    live = [jnp.where(w > 0, 1, 0) for w in weights]
+    factor = [[None] * BLK_DEV for _ in range(CAP)]
+    slot = [0] * CAP
+    rank = 0
+    for k in range(BLK_DEV):
+        for s in range(CAP):
+            hit = live[k] * jnp.where(rank == s, 1, 0)
+            factor[s][k] = hit.astype(F32)
+            slot[s] = slot[s] + hit * weights[k]
+        rank = rank + live[k]
+    return factor, [w.astype(F32) for w in slot]
+
+
+def step_kernel(
+    n,
+    context_ref, residual_ref, proj_ref, head_ref, boot_ref,
+    gctx_ref, gres_ref, gproj_ref, ghead_ref,
+    whole, pool, poolg, msg, xin, nbuf, ng, dg, dxs, dxin, gg, pout, pin, tout, tin,
+    z_send, z_recv, pc_send, pc_recv, pl_send, pl_recv, co_send, co_recv,
+    ms_send, ms_recv, n_send, n_recv, d_send, d_recv, dx_send, dx_recv,
+    g_send, g_recv, r_send, r_recv,
+):
+    group, dp, me = lax.axis_index("groups"), lax.axis_index("dp"), lax.axis_index("member")
+    width = context_ref.shape[1]
+    part = width // n
+    cut = part // 8
+    core = lax.rem(dp, 2)
+    mate = dp + 1 - 2 * core
+    across = lax.rem(dp + 2, 4)
+    across_mate = lax.rem(mate + 2, 4)
+    other = 1 - group
+
+    def copy(src, dst, send, recv, g=None, d=None, m=None):
+        return pltpu.make_async_remote_copy(
+            src_ref=src, dst_ref=dst, send_sem=send, recv_sem=recv,
+            device_id=(group if g is None else g, dp if d is None else d, me if m is None else m),
+            device_id_type=MESH,
+        )
+
+    def piece(owner, g, d):
+        return pl.ds(pl.multiple_of(owner * part + (g * 4 + d) * cut, cut), cut)
+
+    def cols(index):
+        return pl.ds(pl.multiple_of(index * part, part), part)
+
+    barrier = pltpu.get_barrier_semaphore()
+    peers = [(group, dp, lax.rem(me + r, n)) for r in range(1, n)]
+    peers += [(group, d, me) for d in (mate, across, across_mate)]
+    peers += [(other, d, me) for d in (dp, across)]
+    for peer in peers:
+        pl.semaphore_signal(barrier, inc=1, device_id=peer, device_id_type=MESH)
+
+    tokens = context_ref.shape[0]
+    first = lax.broadcasted_iota(jnp.int32, (ROW_DEV, tokens), 0) * 2
+    gap = lax.broadcasted_iota(jnp.int32, (ROW_DEV, tokens), 1) - first
+    pair = jnp.where((gap >= 0) & (gap < 2), 1.0, 0.0).astype(BF16)
+    pool[...] = jnp.dot(pair, context_ref[...], preferred_element_type=F32).astype(BF16)
+    pl.semaphore_wait(barrier, len(peers))
+
+    own_piece = pl.ds(pl.multiple_of((group * 4 + dp) * cut, cut), cut)
+    pending = []
+    for r in range(1, n):
+        z = copy(proj_ref.at[own_piece], whole.at[piece(me, group, dp)], z_send.at[r - 1], z_recv.at[r - 1],
+                 m=lax.rem(me + r, n))
+        z.start()
+        pending.append(z)
+    pool_copies = []
+    for r in range(1, n):
+        c = copy(pool.at[:, cols(lax.rem(me + r, n))], poolg.at[me], pc_send.at[r - 1], pc_recv.at[r - 1],
+                 m=lax.rem(me + r, n))
+        c.start()
+        pool_copies.append(c)
+    poolg[me] = pool[:, cols(me)]
+    whole[cols(me), :] = proj_ref[...]
+    total = jnp.dot(pair, residual_ref[...], preferred_element_type=F32)
+    total += jnp.dot(pool[:, cols(me)], proj_ref[...], preferred_element_type=F32)
+
+    spots = [(group, across), (other, dp), (other, across)]
+    order = [1, n - 1] + list(range(2, n - 1))
+    plane, sides = {}, {}
+    for r in order:
+        owner = lax.rem(me + n - r, n)
+        pending[r - 1].wait_recv()
+        here = whole.at[piece(owner, group, dp)]
+        for t, (g, d) in enumerate(spots):
+            plane[r, t] = copy(here, here, pl_send.at[r - 1, t], pl_recv.at[r - 1, t], g=g, d=d)
+            plane[r, t].start()
+        sides[r, 3] = copy(here, here, co_send.at[r - 1, 3], co_recv.at[r - 1, 3], d=mate)
+        sides[r, 3].start()
+    for r in order:
+        owner = lax.rem(me + n - r, n)
+        for t, (g, d) in enumerate(spots):
+            plane[r, t].wait_recv()
+            there = whole.at[piece(owner, g, d)]
+            sides[r, t] = copy(there, there, co_send.at[r - 1, t], co_recv.at[r - 1, t], d=mate)
+            sides[r, t].start()
+    for r in order:
+        owner = lax.rem(me + n - r, n)
+        for t in range(4):
+            sides[r, t].wait_recv()
+        total += jnp.dot(pool[:, cols(owner)], whole[cols(owner), :], preferred_element_type=F32)
+    latent = (total * 0.5).astype(BF16).astype(F32)
+
+    factors = []
+    sends = []
+    for r in list(range(1, n)) + [0]:
+        head = lax.rem(me + r, n)
+        factor, slot = picks(boot_ref, head)
+        factors.append((head, factor))
+        for s in range(CAP):
+            rows = slice(s * BLOCK, (s + 1) * BLOCK)
+            block = factor[s][0] * latent[:BLOCK]
+            for k in range(1, BLK_DEV):
+                block += factor[s][k] * latent[k * BLOCK : (k + 1) * BLOCK]
+            scale = jnp.zeros((BLOCK, LANES), F32) + slot[s]
+            if r:
+                msg[r - 1, rows, :width] = block.astype(BF16)
+                msg[r - 1, rows, width:] = scale.astype(BF16)
+            else:
+                xin[me, rows, :width] = block.astype(BF16)
+                xin[me, rows, width:] = scale.astype(BF16)
+        if r:
+            c = copy(msg.at[r - 1], xin.at[me], ms_send.at[r - 1], ms_recv.at[r - 1], m=head)
+            c.start()
+            sends.append(c)
+    for c in sends:
+        c.wait_recv()
+
+    count = n * ROW_SLOT
+    x = xin[:, :, :width].reshape(count, width).astype(F32)
+    scale = xin[:, :, width:].reshape(count, LANES).astype(F32)[:, :1] / n
+    inverse = lax.rsqrt(jnp.mean(x * x, axis=-1, keepdims=True) + EPS)
+    normed = x * inverse
+    nbuf[0] = normed.astype(BF16)
+    ng[dp] = nbuf[0, :, pl.ds(pl.multiple_of(dp * (width // 4), width // 4), width // 4)]
+    n_copies = []
+    for t, d in enumerate((across, across_mate, mate)):
+        c = copy(nbuf.at[0, :, pl.ds(pl.multiple_of(d * (width // 4), width // 4), width // 4)], ng.at[dp],
+                 n_send.at[t], n_recv.at[t], d=d)
+        c.start()
+        n_copies.append(c)
+    pre = jnp.dot(nbuf[0], head_ref[0], preferred_element_type=F32)
+    root, cubic = 0.7978845608028654, 0.044715
+    bent = jnp.tanh(root * (pre + cubic * pre * pre * pre))
+    active = 0.5 * pre * (1.0 + bent)
+    slope = 0.5 * (1.0 + bent) + 0.5 * pre * (1.0 - bent * bent) * (root * (1.0 + 3.0 * cubic * pre * pre))
+    place = lax.broadcasted_iota(jnp.int32, (count, 1), 0)
+    keep = jnp.where((place & (BLOCK - 1)) == BLOCK - 1, 0.0, 1.0)
+    after = pltpu.roll(x, count - 1, 0)
+    d_pred = (x + active - after) * (scale * keep)
+    dg[dp] = (d_pred * slope).astype(BF16)
+    d_copies = []
+    for t, d in enumerate((across, mate)):
+        c = copy(dg.at[dp], dg.at[dp], d_send.at[t], d_recv.at[t], d=d)
+        c.start()
+        d_copies.append(c)
+    d_normed = lax.dot_general(dg[dp], head_ref[0], (((1,), (1,)), ((), ())), preferred_element_type=F32)
+    d_rows = d_pred + inverse * (d_normed - normed * jnp.mean(d_normed * normed, axis=-1, keepdims=True))
+    dxs[...] = d_rows.astype(BF16).reshape(n, ROW_SLOT, width)
+    dxin[me] = dxs[me]
+    dx_copies = []
+    for r in range(1, n):
+        peer = lax.rem(me + r, n)
+        c = copy(dxs.at[peer], dxin.at[me], dx_send.at[r - 1], dx_recv.at[r - 1], m=peer)
+        c.start()
+        dx_copies.append(c)
+    d_copies[0].wait_recv()
+    forward = copy(dg.at[across], dg.at[across], d_send.at[2], d_recv.at[2], d=mate)
+    forward.start()
+    for c in dx_copies:
+        c.wait_recv()
+
+    rows = [jnp.zeros((BLOCK, width), F32) for _ in range(BLK_DEV)]
+    for head, factor in factors:
+        back = dxin[head].astype(F32)
+        for k in range(BLK_DEV):
+            for s in range(CAP):
+                rows[k] += factor[s][k] * back[s * BLOCK : (s + 1) * BLOCK]
+    for k in range(BLK_DEV):
+        gg[me, k * BLOCK : (k + 1) * BLOCK, :] = (rows[k] * (1.0 / POOL)).astype(BF16)
+    g_copies = []
+    for r in range(1, n):
+        c = copy(gg.at[me], gg.at[me], g_send.at[r - 1], g_recv.at[r - 1], m=lax.rem(me + r, n))
+        c.start()
+        g_copies.append(c)
+
+    repeat = lax.broadcasted_iota(jnp.int32, (tokens, ROW_DEV), 1) * 2
+    gap = lax.broadcasted_iota(jnp.int32, (tokens, ROW_DEV), 0) - repeat
+    spread = jnp.where((gap >= 0) & (gap < 2), 1.0, 0.0).astype(BF16)
+    grad = gg[me]
+    gres_ref[...] = jnp.dot(spread, grad, preferred_element_type=F32).astype(BF16)
+    gctx = lax.dot_general(grad, whole[...], (((1,), (1,)), ((), ())), preferred_element_type=F32)
+    gctx_ref[...] = jnp.dot(spread, gctx.astype(BF16), preferred_element_type=F32).astype(BF16)
+    for c in n_copies:
+        c.wait_recv()
+    d_copies[1].wait_recv()
+    forward.wait_recv()
+    ghead_ref[0] = lax.dot_general(
+        ng[...].reshape(4 * count, width // 4), dg[...].reshape(4 * count, width),
+        (((0,), (0,)), ((), ())), preferred_element_type=F32)
+
+    for c in pool_copies:
+        c.wait_recv()
+    for c in g_copies:
+        c.wait_recv()
+    half = part // 2
+    mine = pl.ds(pl.multiple_of(core * half, half), half)
+    theirs = pl.ds(pl.multiple_of((1 - core) * half, half), half)
+    gproj_ref[...] = lax.dot_general(
+        poolg[...].reshape(n * ROW_DEV, part), gg[...].reshape(n * ROW_DEV, width),
+        (((0,), (0,)), ((), ())), preferred_element_type=F32)
+    pout[...] = gproj_ref[theirs, :].astype(BF16)
+    a = copy(pout, pin, r_send.at[0], r_recv.at[0], d=mate)
+    a.start()
+    a.wait_recv()
+    tout[...] = (gproj_ref[mine, :] + pin[...].astype(F32)).astype(BF16)
+    b = copy(tout, tin, r_send.at[1], r_recv.at[1], d=across)
+    b.start()
+    b.wait_recv()
+    gproj_ref[mine, :] = tout[...].astype(F32) + tin[...].astype(F32)
+    c = copy(gproj_ref.at[mine], gproj_ref.at[mine], r_send.at[2], r_recv.at[2], d=mate)
+    c.start()
+    c.wait_recv()
+    for copies in (pending, pool_copies, plane.values(), sides.values(), sends, n_copies, d_copies, dx_copies, g_copies):
+        for c2 in copies:
+            c2.wait_send()
+    for c2 in (forward, a, b, c):
+        c2.wait_send()
+
+
+def fused(context, residual, proj_weight, head_weights, boot):
+    n = lax.axis_size("member")
+    tokens, width = context.shape
+    count = n * ROW_SLOT
+    part = width // n
+    vmem = pl.BlockSpec(memory_space=pltpu.VMEM)
+    dma = pltpu.SemaphoreType.DMA
+    peer = dma((n - 1,))
+    return pl.pallas_call(
+        functools.partial(step_kernel, n),
+        out_shape=(
+            jax.ShapeDtypeStruct((tokens, width), BF16),
+            jax.ShapeDtypeStruct((tokens, width), BF16),
+            jax.ShapeDtypeStruct((part, width), F32),
+            jax.ShapeDtypeStruct((1, width // 4, width), F32),
+        ),
+        in_specs=[vmem] * 4 + [pl.BlockSpec(memory_space=pltpu.SMEM)],
+        out_specs=(vmem,) * 4,
+        scratch_shapes=[
+            pltpu.VMEM((width, width), BF16),
+            pltpu.VMEM((ROW_DEV, width), BF16),
+            pltpu.VMEM((n, ROW_DEV, part), BF16),
+            pltpu.VMEM((n - 1, ROW_SLOT, width + LANES), BF16),
+            pltpu.VMEM((n, ROW_SLOT, width + LANES), BF16),
+            pltpu.VMEM((1, count, width), BF16),
+            pltpu.VMEM((4, count, width // 4), BF16),
+            pltpu.VMEM((4, count, width), BF16),
+            pltpu.VMEM((n, ROW_SLOT, width), BF16),
+            pltpu.VMEM((n, ROW_SLOT, width), BF16),
+            pltpu.VMEM((n, ROW_DEV, width), BF16),
+            pltpu.VMEM((part // 2, width), BF16),
+            pltpu.VMEM((part // 2, width), BF16),
+            pltpu.VMEM((part // 2, width), BF16),
+            pltpu.VMEM((part // 2, width), BF16),
+            peer, peer, peer, peer,
+            dma((n - 1, 3)), dma((n - 1, 3)), dma((n - 1, 4)), dma((n - 1, 4)),
+            peer, peer, dma((3,)), dma((3,)), dma((3,)), dma((3,)), peer, peer,
+            peer, peer, dma((3,)), dma((3,)),
+        ],
+        compiler_params=pltpu.CompilerParams(
+            collective_id=0, has_side_effects=True, vmem_limit_bytes=56 * 2**20
+        ),
+        name="step",
+    )(context, residual, proj_weight, head_weights, boot)
+
+
 def solution(mesh):
     in_specs = (
         P(("groups", "dp", "member"), None),

time: 216 us -> 72.5 us (0.34)
  waiting for transfers between devices: 151 us -> 0 us
  Pallas kernels: 0 us -> 64.3 us
  blocking collectives: 23 us -> 0 us
  between operations: 14 us -> 0.65 us
  matrix products: 11.8 us -> 0 us
  other arithmetic: 4.83 us -> 0 us
  starting transfers between devices: 3.57 us -> 0 us
    reduce_scatter x2 -> x0, waiting for transfers between devices: 75.3 us -> none  [the longest x1 42.2 us: local(): lax.psum_scatter(lax.dot_general(columns, grad_low, (((0,), (0,)), ((), (...]
    pallas_call x0 -> x1, Pallas kernels: none -> 64.3 us  [fused(): pl.pallas_call(functools.partial(step_kernel, n), out_shape=(jax.ShapeDty...]
    all_gather x1 -> x0, waiting for transfers between devices: 37 us -> none  [local(): whole_proj = lax.all_gather(proj_weight, 'member', axis=0, tiled=True)]
    psum x1 -> x0, waiting for transfers between devices: 32.5 us -> none  [local(): lax.psum(grad_proj.astype(jnp.bfloat16), 'dp').astype(jnp.float32)]
    all_gather x2 -> x0, blocking collectives: 23 us -> none  [the longest x1 12.5 us: local(): lax.all_gather(latent, 'member', axis=0, tiled=True)]
    dot_general x8 -> x0, matrix products: 11.8 us -> none  [the longest x1 3.13 us: local(): lax.dot_general(grad_low, whole_proj, (((1,), (1,)), ((), ())), preferred...]
    all_to_all x1 -> x0, waiting for transfers between devices: 5.16 us -> none  [local(): lax.all_to_all(d_rows, 'member', split_axis=0, concat_axis=0, tiled=True)]
    unnamed x9 -> x6, local copies, waits for them, and re-layouts: 3.09 us -> 6.71 us
  transfers between devices with their start and end apart: 5 -> 0, of which waited for: 5 -> 0; matrix products, arithmetic and copies ran while one was open for 4% -> 0% of each run, Pallas kernels for 0% -> 0%
where the time goes in v1:
time: 72.5 us; the launch traced here: 71.6 us
  Pallas kernels  64.3 us (89%)
  local copies, waits for them, and re-layouts  6.71 us (9%)
    pallas_call x1, Pallas kernels, fused(): pl.pallas_call(functools.partial(step_kernel, n), out_shape=(jax.ShapeDty...  64.3 us
    unnamed x6, local copies, waits for them, and re-layouts  6.71 us

profile of v1, /device:TPU:1, one launch (start us, length us, event | category | flops | bytes accessed | tf_op | source)
XLA Modules:
  0.0 71.6 jit_solution(18335547739520400589)
XLA Ops:
  0.6 64.3 %step.1 = (bf16[128,1024]{1,0:T(8,128)(2,1)}, bf16[128,1024]{1,0:T(8,128)(2,1)}, f32[256,1024]{1,0:T(8,128)}, f32[1,256,1024]{2,1,0:T(8,128)}) custom-call(bf16[128,1024]{1,0:T(8,128)(2,1)} %context_ref.1, bf16[128,1024]{1,0:T(8,128)(2,1)} %residual_ref.1, bf16[256,1024]{1,0:T(8,128)(2,1)} %proj_ref.1, bf16[1,1024,1024]{2,1,0:T(8,128)(2,1)} %head_ref.1, ...), custom_call_target="tpu_custom_call" | custom-call | tf_op jit(solution)/shard_map/step/pallas_call | solution.py:376
  64.9 0.0 copy-start
  64.9 1.8 %copy.13 = bf16[128,1024]{1,0:T(8,128)(2,1)} copy(bf16[128,1024]{1,0:T(8,128)(2,1)} %get-tuple-element.8) | data formatting | bytes 524288
  66.7 1.7 %copy.14 = bf16[128,1024]{1,0:T(8,128)(2,1)} copy(bf16[128,1024]{1,0:T(8,128)(2,1)} %get-tuple-element.9) | data formatting | bytes 524288
  68.3 2.3 %copy.15 = f32[256,1024]{1,0:T(8,128)} copy(f32[256,1024]{1,0:T(8,128)} %get-tuple-element.10) | data formatting | bytes 2097152
  70.6 0.0 copy-done
  70.6 1.0 %copy.16 = f32[1,256,1024]{2,1,0:T(8,128)} copy(f32[1,256,1024]{2,1,0:T(8,128)S(1)} %copy-done) | data formatting | bytes 2097152
Async XLA Ops:
  64.9 5.7 %copy-start = (f32[1,256,1024]{2,1,0:T(8,128)S(1)}, f32[1,256,1024]{2,1,0:T(8,128)}, u32[]{:S(2)}) copy-start(f32[1,256,1024]{2,1,0:T(8,128)} %get-tuple-element.11) | copy-start | bytes 3145732

commit v2 on v0

--- a/solution.py
+++ b/solution.py
@@ -1,6 +1,10 @@
+import functools
+
 import jax
 import jax.numpy as jnp
 from jax import lax
+from jax.experimental import pallas as pl
+from jax.experimental.pallas import tpu as pltpu
 from jax.sharding import PartitionSpec as P
 
 POOL = 2
@@ -53,6 +57,9 @@
 
 def local(context, residual, proj_weight, head_weights, boot):
     members = lax.axis_size("member")
+    fits = lax.axis_size("dp") == 4 and lax.axis_size("groups") == 2
+    if fits and boot.shape[1] == members == 4 and context.shape[1] % (256 * members) == 0:
+        return fused(context, residual, proj_weight, head_weights, boot)
     head_count = boot.shape[1]
     model_width = context.shape[1]
     own_index = lax.axis_index("member")
@@ -118,6 +125,338 @@
     return (grad_context.astype(jnp.bfloat16), grad_low, grad_proj, grad_head[None])
 
 
+MESH = pl.DeviceIdType.MESH
+F32 = jnp.float32
+BF16 = jnp.bfloat16
+LANES = 128
+ROW_DEV = BLK_DEV * BLOCK
+ROW_SLOT = CAP * BLOCK
+
+
+def picks(boot_ref, head):
+    weights = [boot_ref[k, head] for k in range(BLK_DEV)]
+    live = [jnp.where(w > 0, 1, 0) for w in weights]
+    factor = [[None] * BLK_DEV for _ in range(CAP)]
+    slot = [0] * CAP
+    rank = 0
+    for k in range(BLK_DEV):
+        for s in range(CAP):
+            hit = live[k] * jnp.where(rank == s, 1, 0)
+            factor[s][k] = hit.astype(F32)
+            slot[s] = slot[s] + hit * weights[k]
+        rank = rank + live[k]
+    return factor, [w.astype(F32) for w in slot]
+
+
+def step_kernel(
+    n,
+    context_hbm, residual_hbm, proj_hbm, head_hbm, boot_ref,
+    gctx_ref, gres_ref, gproj_ref, ghead_ref,
+    context_ref, residual_ref, head_ref,
+    whole, pool, poolg, msg, xin, nbuf, ng, dg, dxs, dxin, gg,
+    in_sem, z_send, z_recv, pc_send, pc_recv, pf_send, pf_recv, pl_send, pl_recv, co_send, co_recv,
+    ms_send, ms_recv, n_send, n_recv, d_send, d_recv, dx_send, dx_recv,
+    g_send, g_recv, gx_send, gx_recv, gm_send, gm_recv,
+):
+    group, dp, me = lax.axis_index("groups"), lax.axis_index("dp"), lax.axis_index("member")
+    tokens, width = context_ref.shape
+    part = width // n
+    cut = part // 8
+    core = lax.rem(dp, 2)
+    mate = dp + 1 - 2 * core
+    across = lax.rem(dp + 2, 4)
+    across_mate = lax.rem(mate + 2, 4)
+    other = 1 - group
+    near = [me + 1 - 2 * lax.rem(me, 2), 2 - me // 2, 3 - 3 * (me // 2)]
+    flight = []
+
+    def copy(src, dst, send, recv, g=None, d=None, m=None):
+        made = pltpu.make_async_remote_copy(
+            src_ref=src, dst_ref=dst, send_sem=send, recv_sem=recv,
+            device_id=(group if g is None else g, dp if d is None else d, me if m is None else m),
+            device_id_type=MESH,
+        )
+        made.start()
+        flight.append(made)
+        return made
+
+    def arrival(dst, send, recv):
+        pltpu.make_async_remote_copy(
+            src_ref=dst, dst_ref=dst, send_sem=send, recv_sem=recv,
+            device_id=(group, mate, me), device_id_type=MESH,
+        ).wait_recv()
+
+    def rows_of(owner, g, d, low=0, high=None):
+        high = cut if high is None else high
+        return pl.ds(pl.multiple_of(owner * part + (g * 4 + d) * cut + low, high - low), high - low)
+
+    def cols(index):
+        return pl.ds(pl.multiple_of(index * part, part), part)
+
+    barrier = pltpu.get_barrier_semaphore()
+    peers = [(group, dp, m) for m in near]
+    peers += [(group, d, me) for d in (mate, across, across_mate)]
+    peers += [(other, dp, me)]
+    for peer in peers:
+        pl.semaphore_signal(barrier, inc=1, device_id=peer, device_id_type=MESH)
+    loads = [
+        pltpu.make_async_copy(context_hbm, context_ref, in_sem.at[0]),
+        pltpu.make_async_copy(residual_hbm, residual_ref, in_sem.at[1]),
+        pltpu.make_async_copy(proj_hbm, whole.at[cols(me)], in_sem.at[2]),
+        pltpu.make_async_copy(head_hbm.at[0], head_ref, in_sem.at[3]),
+    ]
+    for load in loads[:3]:
+        load.start()
+    pl.semaphore_wait(barrier, len(peers))
+
+    own_piece = pl.ds(pl.multiple_of((group * 4 + dp) * cut, cut), cut)
+    for i, m in enumerate(near):
+        copy(proj_hbm.at[own_piece], whole.at[rows_of(me, group, dp)], z_send.at[i], z_recv.at[me], m=m)
+    loads[3].start()
+    loads[0].wait()
+    loads[1].wait()
+    first = lax.broadcasted_iota(jnp.int32, (ROW_DEV, tokens), 0) * 2
+    gap = lax.broadcasted_iota(jnp.int32, (ROW_DEV, tokens), 1) - first
+    pair = jnp.where((gap >= 0) & (gap < 2), 1.0, 0.0).astype(BF16)
+    pool[...] = jnp.dot(pair, context_ref[...], preferred_element_type=F32).astype(BF16)
+    poolg[dp, me] = pool[:, cols(me)]
+
+    half = cut // 2
+    for i, owner in enumerate(near):
+        here = whole.at[rows_of(owner, group, dp)]
+        arrival(here, z_send.at[i], z_recv.at[owner])
+        copy(here, here, pl_send.at[i, 0], pl_recv.at[owner, 0], d=across)
+        copy(here, here, pl_send.at[i, 1], pl_recv.at[owner, 1], g=other)
+        copy(here, here, co_send.at[i, 0], co_recv.at[owner, 0], d=mate)
+    for i, m in enumerate(near):
+        copy(pool.at[:, cols(m)], poolg.at[dp, me], pc_send.at[i], pc_recv.at[me], m=m)
+    loads[2].wait()
+    total = jnp.dot(pair, residual_ref[...], preferred_element_type=F32)
+    total += jnp.dot(pool[:, cols(me)], whole[cols(me), :], preferred_element_type=F32)
+    for i, owner in enumerate(near):
+        there = whole.at[rows_of(owner, group, across)]
+        arrival(there, pl_send.at[i, 0], pl_recv.at[owner, 0])
+        low = whole.at[rows_of(owner, group, across, 0, half)]
+        copy(low, low, pl_send.at[i, 2], pl_recv.at[owner, 2], g=other)
+        copy(there, there, co_send.at[i, 1], co_recv.at[owner, 1], d=mate)
+        there = whole.at[rows_of(owner, other, dp)]
+        arrival(there, pl_send.at[i, 1], pl_recv.at[owner, 1])
+        high = whole.at[rows_of(owner, other, dp, half, cut)]
+        copy(high, high, pl_send.at[i, 3], pl_recv.at[owner, 3], d=across)
+        copy(there, there, co_send.at[i, 2], co_recv.at[owner, 2], d=mate)
+    for i, owner in enumerate(near):
+        arrival(whole.at[rows_of(owner, other, across, 0, half)], pl_send.at[i, 2], pl_recv.at[owner, 2])
+        arrival(whole.at[rows_of(owner, other, across, half, cut)], pl_send.at[i, 3], pl_recv.at[owner, 3])
+        there = whole.at[rows_of(owner, other, across)]
+        copy(there, there, co_send.at[i, 3], co_recv.at[owner, 3], d=mate)
+    for i, owner in enumerate(near):
+        for t, (g, d) in enumerate(((group, mate), (group, across_mate), (other, mate), (other, across_mate))):
+            arrival(whole.at[rows_of(owner, g, d)], co_send.at[i, t], co_recv.at[owner, t])
+        total += jnp.dot(pool[:, cols(owner)], whole[cols(owner), :], preferred_element_type=F32)
+    latent = (total * 0.5).astype(BF16).astype(F32)
+
+    factors = []
+    for i, head in list(enumerate(near))[::-1] + [(-1, me)]:
+        factor, slot = picks(boot_ref, head)
+        factors.append((head, factor))
+        for s in range(CAP):
+            rows = slice(s * BLOCK, (s + 1) * BLOCK)
+            block = factor[s][0] * latent[:BLOCK]
+            for k in range(1, BLK_DEV):
+                block += factor[s][k] * latent[k * BLOCK : (k + 1) * BLOCK]
+            scale = jnp.zeros((BLOCK, LANES), F32) + slot[s]
+            if i >= 0:
+                msg[i, rows, :width] = block.astype(BF16)
+                msg[i, rows, width:] = scale.astype(BF16)
+            else:
+                xin[me, rows, :width] = block.astype(BF16)
+                xin[me, rows, width:] = scale.astype(BF16)
+        if i >= 0:
+            copy(msg.at[i], xin.at[me], ms_send.at[i], ms_recv.at[me], m=head)
+
+    for i, m in enumerate(near):
+        arrival(poolg.at[dp, m], pc_send.at[i], pc_recv.at[m])
+    copy(poolg.at[dp], poolg.at[dp], pf_send.at[0], pf_recv.at[0], d=across)
+    copy(poolg.at[dp], poolg.at[dp], pf_send.at[1], pf_recv.at[1], d=mate)
+    for i, m in enumerate(near):
+        arrival(xin.at[m], ms_send.at[i], ms_recv.at[m])
+
+    count = n * ROW_SLOT
+    x = xin[:, :, :width].reshape(count, width).astype(F32)
+    scale = xin[:, :, width:].reshape(count, LANES).astype(F32)[:, :1] / n
+    inverse = lax.rsqrt(jnp.mean(x * x, axis=-1, keepdims=True) + EPS)
+    normed = x * inverse
+    nbuf[...] = normed.astype(BF16)
+
+    def quarter(d):
+        return pl.ds(pl.multiple_of(d * (width // 4), width // 4), width // 4)
+
+    ng[dp] = nbuf[:, quarter(dp)]
+    for t, d in enumerate((across, across_mate, mate)):
+        copy(nbuf.at[:, quarter(d)], ng.at[dp], n_send.at[t], n_recv.at[t], d=d)
+    loads[3].wait()
+    pre = jnp.dot(nbuf[...], head_ref[...], preferred_element_type=F32)
+    root, cubic = 0.7978845608028654, 0.044715
+    bent = jnp.tanh(root * (pre + cubic * pre * pre * pre))
+    active = 0.5 * pre * (1.0 + bent)
+    slope = 0.5 * (1.0 + bent) + 0.5 * pre * (1.0 - bent * bent) * (root * (1.0 + 3.0 * cubic * pre * pre))
+    place = lax.broadcasted_iota(jnp.int32, (count, 1), 0)
+    keep = jnp.where((place & (BLOCK - 1)) == BLOCK - 1, 0.0, 1.0)
+    after = pltpu.roll(x, count - 1, 0)
+    d_pred = (x + active - after) * (scale * keep)
+    dg[dp] = (d_pred * slope).astype(BF16)
+    copy(dg.at[dp], dg.at[dp], d_send.at[0], d_recv.at[0], d=across)
+    copy(dg.at[dp], dg.at[dp], d_send.at[1], d_recv.at[1], d=mate)
+    d_normed = lax.dot_general(dg[dp], head_ref[...], (((1,), (1,)), ((), ())), preferred_element_type=F32)
+    d_rows = d_pred + inverse * (d_normed - normed * jnp.mean(d_normed * normed, axis=-1, keepdims=True))
+    dxs[...] = d_rows.astype(BF16).reshape(n, ROW_SLOT, width)
+    dxin[me] = dxs[me]
+    for i, m in list(enumerate(near))[::-1]:
+        copy(dxs.at[m], dxin.at[me], dx_send.at[i], dx_recv.at[me], m=m)
+    arrival(poolg.at[across], pf_send.at[0], pf_recv.at[0])
+    copy(poolg.at[across], poolg.at[across], pf_send.at[2], pf_recv.at[2], d=mate)
+    arrival(dg.at[across], d_send.at[0], d_recv.at[0])
+    copy(dg.at[across], dg.at[across], d_send.at[2], d_recv.at[2], d=mate)
+    for i, m in enumerate(near):
+        arrival(dxin.at[m], dx_send.at[i], dx_recv.at[m])
+
+    rows = [jnp.zeros((BLOCK, width), F32) for _ in range(BLK_DEV)]
+    for head, factor in factors:
+        back = dxin[head].astype(F32)
+        for k in range(BLK_DEV):
+            for s in range(CAP):
+                rows[k] += factor[s][k] * back[s * BLOCK : (s + 1) * BLOCK]
+    for k in range(BLK_DEV):
+        gg[dp, me, k * BLOCK : (k + 1) * BLOCK, :] = (rows[k] * (1.0 / POOL)).astype(BF16)
+    own = gg.at[dp, me]
+    for i, m in enumerate(near):
+        copy(own, own, g_send.at[i], g_recv.at[me], m=m)
+    copy(own, own, gx_send.at[n - 1], gx_recv.at[me], d=across)
+    copy(own, own, gm_send.at[0, n - 1], gm_recv.at[0, me], d=mate)
+
+    grad = gg[dp, me]
+    gres_ref[...] = grad
+    gctx = lax.dot_general(grad, whole[...], (((1,), (1,)), ((), ())), preferred_element_type=F32)
+    gctx_ref[...] = gctx.astype(BF16)
+
+    def relay(i, m):
+        block = gg.at[dp, m]
+        arrival(block, g_send.at[i], g_recv.at[m])
+        copy(block, block, gx_send.at[i], gx_recv.at[m], d=across)
+        copy(block, block, gm_send.at[0, i], gm_recv.at[0, m], d=mate)
+
+    def relay_across(i, m):
+        block = gg.at[across, m]
+        arrival(block, gx_send.at[i], gx_recv.at[m])
+        copy(block, block, gm_send.at[1, i], gm_recv.at[1, m], d=mate)
+
+    relay(0, near[0])
+    for t, d in enumerate((across, across_mate, mate)):
+        arrival(ng.at[d], n_send.at[t], n_recv.at[t])
+    arrival(dg.at[mate], d_send.at[1], d_recv.at[1])
+    arrival(dg.at[across_mate], d_send.at[2], d_recv.at[2])
+    ghead_ref[0] = lax.dot_general(
+        ng[...].reshape(4 * count, width // 4), dg[...].reshape(4 * count, width),
+        (((0,), (0,)), ((), ())), preferred_element_type=F32)
+    relay(1, near[1])
+    relay_across(n - 1, me)
+    relay_across(0, near[0])
+    relay(2, near[2])
+    relay_across(1, near[1])
+    relay_across(2, near[2])
+
+    arrival(poolg.at[mate], pf_send.at[1], pf_recv.at[1])
+    arrival(poolg.at[across_mate], pf_send.at[2], pf_recv.at[2])
+    for i, m in enumerate(list(near) + [me]):
+        arrival(gg.at[mate, m], gm_send.at[0, i], gm_recv.at[0, m])
+        arrival(gg.at[across_mate, m], gm_send.at[1, i], gm_recv.at[1, m])
+    gproj_ref[...] = lax.dot_general(
+        poolg[...].reshape(4 * n * ROW_DEV, part), gg[...].reshape(4 * n * ROW_DEV, width),
+        (((0,), (0,)), ((), ())), preferred_element_type=F32)
+    for made in flight:
+        made.wait_send()
+
+
+def finish_kernel(gctx_in, gres_in, gproj_in, ghead_in, gctx_out, gres_out, gproj_out, ghead_out, wide, sem):
+    moves = [
+        pltpu.make_async_copy(ghead_in, ghead_out, sem.at[0]),
+        pltpu.make_async_copy(gproj_in, gproj_out, sem.at[1]),
+    ]
+    for move in moves:
+        move.start()
+    rows = gres_in.shape[0]
+    start = lax.broadcasted_iota(jnp.int32, (rows * POOL, rows), 1) * POOL
+    gap = lax.broadcasted_iota(jnp.int32, (rows * POOL, rows), 0) - start
+    spread = jnp.where((gap >= 0) & (gap < POOL), 1.0, 0.0).astype(BF16)
+    for i, (src, dst) in enumerate(((gres_in, gres_out), (gctx_in, gctx_out))):
+        wide[i] = jnp.dot(spread, src[...], preferred_element_type=F32).astype(BF16)
+        move = pltpu.make_async_copy(wide.at[i], dst, sem.at[2 + i])
+        move.start()
+        moves.append(move)
+    for move in moves:
+        move.wait()
+
+
+def fused(context, residual, proj_weight, head_weights, boot):
+    n = lax.axis_size("member")
+    tokens, width = context.shape
+    count = n * ROW_SLOT
+    part = width // n
+    hbm = pl.BlockSpec(memory_space=pltpu.HBM)
+    vmem = pl.BlockSpec(memory_space=pltpu.VMEM)
+    dma = pltpu.SemaphoreType.DMA
+    peer, owner = dma((n - 1,)), dma((n,))
+    partial = pl.pallas_call(
+        functools.partial(step_kernel, n),
+        out_shape=(
+            pltpu.VMEM((ROW_DEV, width), BF16),
+            pltpu.VMEM((ROW_DEV, width), BF16),
+            pltpu.VMEM((part, width), F32),
+            pltpu.VMEM((1, width // 4, width), F32),
+        ),
+        in_specs=[hbm] * 4 + [pl.BlockSpec(memory_space=pltpu.SMEM)],
+        out_specs=(vmem,) * 4,
+        scratch_shapes=[
+            pltpu.VMEM((tokens, width), BF16),
+            pltpu.VMEM((tokens, width), BF16),
+            pltpu.VMEM((width, width), BF16),
+            pltpu.VMEM((width, width), BF16),
+            pltpu.VMEM((ROW_DEV, width), BF16),
+            pltpu.VMEM((4, n, ROW_DEV, part), BF16),
+            pltpu.VMEM((n - 1, ROW_SLOT, width + LANES), BF16),
+            pltpu.VMEM((n, ROW_SLOT, width + LANES), BF16),
+            pltpu.VMEM((count, width), BF16),
+            pltpu.VMEM((4, count, width // 4), BF16),
+            pltpu.VMEM((4, count, width), BF16),
+            pltpu.VMEM((n, ROW_SLOT, width), BF16),
+            pltpu.VMEM((n, ROW_SLOT, width), BF16),
+            pltpu.VMEM((4, n, ROW_DEV, width), BF16),
+            dma((4,)), peer, owner, peer, owner, dma((3,)), dma((3,)),
+            dma((n - 1, 4)), dma((n, 4)), dma((n - 1, 4)), dma((n, 4)),
+            peer, owner, dma((3,)), dma((3,)), dma((3,)), dma((3,)), peer, owner,
+            peer, owner, owner, owner, dma((2, n)), dma((2, n)),
+        ],
+        compiler_params=pltpu.CompilerParams(
+            collective_id=0, has_side_effects=True, vmem_limit_bytes=62900 * 2**10
+        ),
+        name="step",
+    )(context, residual, proj_weight, head_weights, boot)
+    return pl.pallas_call(
+        finish_kernel,
+        out_shape=(
+            jax.ShapeDtypeStruct((tokens, width), BF16),
+            jax.ShapeDtypeStruct((tokens, width), BF16),
+            jax.ShapeDtypeStruct((part, width), F32),
+            jax.ShapeDtypeStruct((1, width // 4, width), F32),
+        ),
+        in_specs=[vmem] * 4,
+        out_specs=(hbm,) * 4,
+        scratch_shapes=[pltpu.VMEM((2, tokens, width), BF16), dma((4,))],
+        compiler_params=pltpu.CompilerParams(vmem_limit_bytes=16 * 2**20),
+        name="finish",
+    )(*partial)
+
+
 def solution(mesh):
     in_specs = (
         P(("groups", "dp", "member"), None),

time: 216 us -> 64.6 us (0.30)
  waiting for transfers between devices: 151 us -> 0 us
  Pallas kernels: 0 us -> 63.8 us
  blocking collectives: 23 us -> 0 us
  between operations: 14 us -> 0.64 us
  matrix products: 11.8 us -> 0 us
  local copies, waits for them, and re-layouts: 5.98 us -> 0 us
  other arithmetic: 4.83 us -> 0 us
  starting transfers between devices: 3.57 us -> 0 us
    reduce_scatter x2 -> x0, waiting for transfers between devices: 75.3 us -> none  [the longest x1 42.2 us: local(): lax.psum_scatter(lax.dot_general(columns, grad_low, (((0,), (0,)), ((), (...]
    pallas_call x0 -> x2, Pallas kernels: none -> 63.8 us  [the longest x1 62.3 us: fused(): pl.pallas_call(functools.partial(step_kernel, n), out_shape=(pltpu.VMEM((...]
    all_gather x1 -> x0, waiting for transfers between devices: 37 us -> none  [local(): whole_proj = lax.all_gather(proj_weight, 'member', axis=0, tiled=True)]
    psum x1 -> x0, waiting for transfers between devices: 32.5 us -> none  [local(): lax.psum(grad_proj.astype(jnp.bfloat16), 'dp').astype(jnp.float32)]
    all_gather x2 -> x0, blocking collectives: 23 us -> none  [the longest x1 12.5 us: local(): lax.all_gather(latent, 'member', axis=0, tiled=True)]
    dot_general x8 -> x0, matrix products: 11.8 us -> none  [the longest x1 3.13 us: local(): lax.dot_general(grad_low, whole_proj, (((1,), (1,)), ((), ())), preferred...]
    all_to_all x1 -> x0, waiting for transfers between devices: 5.16 us -> none  [local(): lax.all_to_all(d_rows, 'member', split_axis=0, concat_axis=0, tiled=True)]
    all_to_all x1 -> x0, starting transfers between devices: 3.41 us -> none  [local(): lax.all_to_all(d_rows, 'member', split_axis=0, concat_axis=0, tiled=True)]
  transfers between devices with their start and end apart: 5 -> 0, of which waited for: 5 -> 0; matrix products, arithmetic and copies ran while one was open for 4% -> 0% of each run, Pallas kernels for 0% -> 0%
where the time goes in v2:
time: 64.6 us; the launch traced here: 64.5 us
  Pallas kernels  63.8 us (99%)
    pallas_call x1, Pallas kernels, fused(): pl.pallas_call(functools.partial(step_kernel, n), out_shape=(pltpu.VMEM((...  62.3 us
    pallas_call x1, Pallas kernels, fused(): pl.pallas_call(finish_kernel, out_shape=(jax.ShapeDtypeStruct((tokens, wi...  1.52 us

profile of v2, /device:TPU:1, one launch (start us, length us, event | category | flops | bytes accessed | tf_op | source)
XLA Modules:
  0.0 64.5 jit_solution(546742633034516053)
XLA Ops:
  0.6 62.3 %step.1 = (bf16[64,1024]{1,0:T(8,128)(2,1)S(1)}, bf16[64,1024]{1,0:T(8,128)(2,1)S(1)}, f32[256,1024]{1,0:T(8,128)S(1)}, f32[1,256,1024]{2,1,0:T(8,128)S(1)}) custom-call(bf16[128,1024]{1,0:T(8,128)(2,1)} %context_hbm.1, bf16[128,1024]{1,0:T(8,128)(2,1)} %residual_hbm.1, bf16[256,1024]{1,0:T(8,128)(2,1)} %proj_hbm.1, bf16[1,1024,1024]{2,1,0:T(8,128)(2,1)} %head_hbm.1, ...), custom_call_target="tpu_custom_call" | custom-call | tf_op jit(solution)/shard_map/step/pallas_call | solution.py:409
  62.9 1.5 %finish.1 = (bf16[128,1024]{1,0:T(8,128)(2,1)}, bf16[128,1024]{1,0:T(8,128)(2,1)}, f32[256,1024]{1,0:T(8,128)}, f32[1,256,1024]{2,1,0:T(8,128)}) custom-call(bf16[64,1024]{1,0:T(8,128)(2,1)S(1)} %get-tuple-element.8.gctx_in, bf16[64,1024]{1,0:T(8,128)(2,1)S(1)} %get-tuple-element.9.gres_in, f32[256,1024]{1,0:T(8,128)S(1)} %get-tuple-element.10.gproj_in, ...), custom_call_target="tpu_custom_call" | custom-call | tf_op jit(solution)/shard_map/finish/pallas_call | solution.py:444

commit v3 on v2

--- a/solution.py
+++ b/solution.py
@@ -328,53 +328,97 @@
                 rows[k] += factor[s][k] * back[s * BLOCK : (s + 1) * BLOCK]
     for k in range(BLK_DEV):
         gg[dp, me, k * BLOCK : (k + 1) * BLOCK, :] = (rows[k] * (1.0 / POOL)).astype(BF16)
-    own = gg.at[dp, me]
-    for i, m in enumerate(near):
-        copy(own, own, g_send.at[i], g_recv.at[me], m=m)
-    copy(own, own, gx_send.at[n - 1], gx_recv.at[me], d=across)
-    copy(own, own, gm_send.at[0, n - 1], gm_recv.at[0, me], d=mate)
+    inner = (me == 1) | (me == 2)
+    split = ROW_DEV // 2
+    passed = []
+
+    def slab(d, m, h):
+        return gg.at[d, m, h * split : (h + 1) * split]
+
+    def onward(d, m, h, slot, target):
+        block = slab(d, m, h)
+        return pltpu.make_async_remote_copy(
+            src_ref=block, dst_ref=block, send_sem=g_send.at[slot, h], recv_sem=g_recv.at[m, h],
+            device_id=(group, dp, target), device_id_type=MESH)
+
+    def pass_on(*what):
+        passed.append(what)
+        onward(*what).start()
+
+    def spread_dp(i, m, h):
+        block = slab(dp, m, h)
+        copy(block, block, gx_send.at[i, h], gx_recv.at[m, h], d=across)
+        copy(block, block, gm_send.at[0, i, h], gm_recv.at[0, m, h], d=mate)
+
+    def take(i, m):
+        for h in range(2):
+            arrival(slab(dp, m, h), g_send.at[i, h], g_recv.at[m, h])
+
+            @pl.when(inner)
+            def _():
+                pass_on(dp, m, h, 2 + i, near[1] if i == 0 else near[0])
+
+            spread_dp(i, m, h)
+
+    def take_across(i, m):
+        for h in range(2):
+            block = slab(across, m, h)
+            arrival(block, gx_send.at[i, h], gx_recv.at[m, h])
+            copy(block, block, gm_send.at[1, i, h], gm_recv.at[1, m, h], d=mate)
+
+    for h in range(2):
+        block = slab(dp, me, h)
+        copy(block, block, g_send.at[0, h], g_recv.at[me, h], m=near[0])
+
+        @pl.when(inner)
+        def _():
+            pass_on(dp, me, h, 1, near[1])
+
+        spread_dp(n - 1, me, h)
 
     grad = gg[dp, me]
     gres_ref[...] = grad
     gctx = lax.dot_general(grad, whole[...], (((1,), (1,)), ((), ())), preferred_element_type=F32)
     gctx_ref[...] = gctx.astype(BF16)
-
-    def relay(i, m):
-        block = gg.at[dp, m]
-        arrival(block, g_send.at[i], g_recv.at[m])
-        copy(block, block, gx_send.at[i], gx_recv.at[m], d=across)
-        copy(block, block, gm_send.at[0, i], gm_recv.at[0, m], d=mate)
-
-    def relay_across(i, m):
-        block = gg.at[across, m]
-        arrival(block, gx_send.at[i], gx_recv.at[m])
-        copy(block, block, gm_send.at[1, i], gm_recv.at[1, m], d=mate)
-
-    relay(0, near[0])
+    take(0, near[0])
     for t, d in enumerate((across, across_mate, mate)):
         arrival(ng.at[d], n_send.at[t], n_recv.at[t])
     arrival(dg.at[mate], d_send.at[1], d_recv.at[1])
     arrival(dg.at[across_mate], d_send.at[2], d_recv.at[2])
-    ghead_ref[0] = lax.dot_general(
-        ng[...].reshape(4 * count, width // 4), dg[...].reshape(4 * count, width),
-        (((0,), (0,)), ((), ())), preferred_element_type=F32)
-    relay(1, near[1])
-    relay_across(n - 1, me)
-    relay_across(0, near[0])
-    relay(2, near[2])
-    relay_across(1, near[1])
-    relay_across(2, near[2])
+
+    def head_part(q):
+        lanes = slice(q * (width // 4), (q + 1) * (width // 4))
+        ghead_ref[0, :, lanes] = lax.dot_general(
+            ng[...].reshape(4 * count, width // 4), dg[:, :, lanes].reshape(4 * count, width // 4),
+            (((0,), (0,)), ((), ())), preferred_element_type=F32)
+
+    head_part(0)
+    take_across(n - 1, me)
+    head_part(1)
+    take(1, near[1])
+    head_part(2)
+    take_across(0, near[0])
+    head_part(3)
+    take(2, near[2])
+    take_across(1, near[1])
+    take_across(2, near[2])
 
     arrival(poolg.at[mate], pf_send.at[1], pf_recv.at[1])
     arrival(poolg.at[across_mate], pf_send.at[2], pf_recv.at[2])
     for i, m in enumerate(list(near) + [me]):
-        arrival(gg.at[mate, m], gm_send.at[0, i], gm_recv.at[0, m])
-        arrival(gg.at[across_mate, m], gm_send.at[1, i], gm_recv.at[1, m])
+        for h in range(2):
+            arrival(slab(mate, m, h), gm_send.at[0, i, h], gm_recv.at[0, m, h])
+            arrival(slab(across_mate, m, h), gm_send.at[1, i, h], gm_recv.at[1, m, h])
     gproj_ref[...] = lax.dot_general(
         poolg[...].reshape(4 * n * ROW_DEV, part), gg[...].reshape(4 * n * ROW_DEV, width),
         (((0,), (0,)), ((), ())), preferred_element_type=F32)
     for made in flight:
         made.wait_send()
+
+    @pl.when(inner)
+    def _():
+        for what in passed:
+            onward(*what).wait_send()
 
 
 def finish_kernel(gctx_in, gres_in, gproj_in, ghead_in, gctx_out, gres_out, gproj_out, ghead_out, wide, sem):
@@ -434,7 +478,7 @@
             dma((4,)), peer, owner, peer, owner, dma((3,)), dma((3,)),
             dma((n - 1, 4)), dma((n, 4)), dma((n - 1, 4)), dma((n, 4)),
             peer, owner, dma((3,)), dma((3,)), dma((3,)), dma((3,)), peer, owner,
-            peer, owner, owner, owner, dma((2, n)), dma((2, n)),
+            dma((n + 1, 2)), dma((n, 2)), dma((n, 2)), dma((n, 2)), dma((2, n, 2)), dma((2, n, 2)),
         ],
         compiler_params=pltpu.CompilerParams(
             collective_id=0, has_side_effects=True, vmem_limit_bytes=62900 * 2**10

time: 64.6 us -> 60.8 us (0.941)
  Pallas kernels: 63.8 us -> 59.9 us
    pallas_call x1, Pallas kernels: 62.3 us -> 58.4 us  [fused(): pl.pallas_call(functools.partial(step_kernel, n), out_shape=(pltpu.VMEM((...]
where the time goes in v3:
time: 60.8 us; the launch traced here: 60.6 us
  Pallas kernels  59.9 us (99%)
  between operations  0.64 us (1%)
    pallas_call x1, Pallas kernels, fused(): pl.pallas_call(functools.partial(step_kernel, n), out_shape=(pltpu.VMEM((...  58.4 us
    pallas_call x1, Pallas kernels, fused(): pl.pallas_call(finish_kernel, out_shape=(jax.ShapeDtypeStruct((tokens, wi...  1.52 us

profile of v3, /device:TPU:1, one launch (start us, length us, event | category | flops | bytes accessed | tf_op | source)
XLA Modules:
  0.0 60.6 jit_solution(9903310223272195506)
XLA Ops:
  0.6 58.4 %step.1 = (bf16[64,1024]{1,0:T(8,128)(2,1)S(1)}, bf16[64,1024]{1,0:T(8,128)(2,1)S(1)}, f32[256,1024]{1,0:T(8,128)S(1)}, f32[1,256,1024]{2,1,0:T(8,128)S(1)}) custom-call(bf16[128,1024]{1,0:T(8,128)(2,1)} %context_hbm.1, bf16[128,1024]{1,0:T(8,128)(2,1)} %residual_hbm.1, bf16[256,1024]{1,0:T(8,128)(2,1)} %proj_hbm.1, bf16[1,1024,1024]{2,1,0:T(8,128)(2,1)} %head_hbm.1, ...), custom_call_target="tpu_custom_call" | custom-call | tf_op jit(solution)/shard_map/step/pallas_call | solution.py:453
  59.1 1.5 %finish.1 = (bf16[128,1024]{1,0:T(8,128)(2,1)}, bf16[128,1024]{1,0:T(8,128)(2,1)}, f32[256,1024]{1,0:T(8,128)}, f32[1,256,1024]{2,1,0:T(8,128)}) custom-call(bf16[64,1024]{1,0:T(8,128)(2,1)S(1)} %get-tuple-element.8.gctx_in, bf16[64,1024]{1,0:T(8,128)(2,1)S(1)} %get-tuple-element.9.gres_in, f32[256,1024]{1,0:T(8,128)S(1)} %get-tuple-element.10.gproj_in, ...), custom_call_target="tpu_custom_call" | custom-call | tf_op jit(solution)/shard_map/finish/pallas_call | solution.py:488
